TPU v7x, 32 devices: a whole 2x2x4 slice. The times are simulated.
32 devices in a mesh: row: 8 (over z, x), col: 4 (over y, core).
Axes of the slice: x: 2, y: 2, z: 4, core: 2. Of those that a mesh axis runs over, the one named last changes fastest.
Arguments:
- innovations: float32 [64, 16384], P(None, ('row', 'col')), may hold values from -300 to 300
- obs_factors: float32 [64, 16384], P(None, ('row', 'col')), may hold values from -6 to 6
- component: int32 [16384], P(('row', 'col')), may hold values 0 or 1
- obs_error: float32 [16384], P(('row', 'col')), may hold values from 0.5 to 2
- coupling: float32 [2, 2], replicated, may hold values from 0.5 to 2
- tile_slots: int32 [8, 4, 8, 3], P('row', 'col'), may hold values from 0 to 7, as said below
Outputs:
- increment: float32 [64, 16384], P(None, ('row', 'col'))
- residual: float32 [64, 16384], P(None, ('row', 'col'))
Inputs may be any that keep to these rules, and one draw needn't show every extreme that they name: `tile_slots`: each device's slots name distinct (local block row, local block column) pairs; on some device all 8 slots are live; the live flag is 0 or 1; local block rows are below 4 and local block columns below 8.
All inputs are finite; a program needn't handle non-finite values. No bound on the sum of `component` on one device may be relied on, other than what follows from the above.
Results may differ from a plain program's by a relative error of at most 0.0003.
Values sent between devices are 32-bit elements; how exact they have to be, the bound alone decides.
A program may use at most 64 MiB of HBM per device.

v0:
```python
import jax
import jax.numpy as jnp
from jax import lax
from jax.sharding import PartitionSpec as P

TILE = 512
ITERS = 3


length_sq = 12.0


def tile_matrix(left_factors, right_factors, left_labels, right_labels, coupling):
    left_norms = jnp.sum(left_factors * left_factors, axis=0)
    right_norms = jnp.sum(right_factors * right_factors, axis=0)
    products = lax.dot_general(
        left_factors,
        right_factors,
        (((0,), (0,)), ((), ())),
        precision=lax.Precision.HIGHEST,
        preferred_element_type=jnp.float32,
    )
    pair_coupling = (1.0 - left_labels)[:, None] * (
        (1.0 - right_labels)[None, :] * coupling[0, 0] + right_labels[None, :] * coupling[0, 1]
    ) + left_labels[:, None] * (
        (1.0 - right_labels)[None, :] * coupling[1, 0] + right_labels[None, :] * coupling[1, 1]
    )
    return pair_coupling * jnp.exp(
        -(left_norms[:, None] + right_norms[None, :] - 2.0 * products) / length_sq
    )


def take_segment(array, block):
    start = block * TILE
    return lax.dynamic_slice_in_dim(array, start, TILE, array.ndim - 1)


def add_segment(vector, block, values):
    start = block * TILE
    last_axis = vector.ndim - 1
    before = lax.dynamic_slice_in_dim(vector, start, TILE, last_axis)
    return lax.dynamic_update_slice_in_dim(vector, before + values, start, last_axis)


def squares(residual):
    return lax.psum(jnp.sum(residual * residual, axis=1), ("row", "col"))


def shards(innovations, obs_factors, component, obs_error, coupling, tile_slots):
    labels_float = component.astype(jnp.float32)
    row_factors, row_labels = (
        lax.all_gather(obs_factors, "col", axis=1, tiled=True),
        lax.all_gather(labels_float, "col", axis=0, tiled=True),
    )
    column_factors, column_labels = (
        lax.all_gather(obs_factors, "row", axis=1, tiled=True),
        lax.all_gather(labels_float, "row", axis=0, tiled=True),
    )
    slots = tile_slots[0, 0]
    count = slots.shape[0]
    flags = slots[:, 2].astype(jnp.float32)
    rhs_count = innovations.shape[0]

    def make_tile(number):
        row_block = slots[number, 0]
        column_block = slots[number, 1]
        block_matrix = tile_matrix(
            take_segment(row_factors, row_block),
            take_segment(column_factors, column_block),
            take_segment(row_labels, row_block),
            take_segment(column_labels, column_block),
            coupling,
        )
        return block_matrix * flags[number]

    def visit(totals, work):
        result = work(totals)
        return result

    stored = jnp.zeros((count, TILE, TILE), jnp.float32)

    def weigh(number, carry):

        def work(carry):
            row_totals, column_totals, stored = carry
            block_matrix = make_tile(number)
            row_totals = add_segment(row_totals, slots[number, 0], jnp.sum(block_matrix, axis=1))
            column_totals = add_segment(
                column_totals, slots[number, 1], jnp.sum(block_matrix, axis=0)
            )
            stored = lax.dynamic_update_index_in_dim(stored, block_matrix, number, 0)
            return (row_totals, column_totals, stored)

        return visit(carry, work)

    start_carry = (
        jnp.zeros((row_factors.shape[1],), jnp.float32),
        jnp.zeros((column_factors.shape[1],), jnp.float32),
        stored,
    )
    row_totals, column_totals, stored = lax.fori_loop(0, count, weigh, start_carry)
    diagonal = (
        obs_error
        + lax.psum_scatter(row_totals, "col", scatter_dimension=0, tiled=True)
        + lax.psum_scatter(column_totals, "row", scatter_dimension=0, tiled=True)
    )

    def fetch(number):
        block_matrix = lax.dynamic_index_in_dim(stored, number, 0, keepdims=False)
        return block_matrix

    increment = jnp.zeros_like(innovations)
    residual = innovations
    direction = innovations
    norm_now = squares(residual)
    for repeat in range(ITERS):
        column_values = lax.all_gather(direction, "row", axis=1, tiled=True)
        row_values = lax.all_gather(direction, "col", axis=1, tiled=True)

        def sweep(number, carry):

            def work(carry):
                row_image, column_image = carry
                block_matrix = fetch(number)
                row_block = slots[number, 0]
                column_block = slots[number, 1]
                right_part = lax.dot_general(
                    take_segment(column_values, column_block),
                    block_matrix,
                    (((1,), (1,)), ((), ())),
                    precision=lax.Precision.HIGHEST,
                    preferred_element_type=jnp.float32,
                )
                left_part = jnp.dot(
                    take_segment(row_values, row_block),
                    block_matrix,
                    precision=lax.Precision.HIGHEST,
                    preferred_element_type=jnp.float32,
                )
                return (
                    add_segment(row_image, row_block, right_part),
                    add_segment(column_image, column_block, left_part),
                )

            return visit(carry, work)

        start_image = (
            jnp.zeros((rhs_count, row_values.shape[1]), jnp.float32),
            jnp.zeros((rhs_count, column_values.shape[1]), jnp.float32),
        )
        row_image, column_image = lax.fori_loop(0, count, sweep, start_image)
        image = (
            diagonal[None, :] * direction
            + lax.psum_scatter(row_image, "col", scatter_dimension=1, tiled=True)
            + lax.psum_scatter(column_image, "row", scatter_dimension=1, tiled=True)
        )
        alpha = norm_now / lax.psum(jnp.sum(direction * image, axis=1), ("row", "col"))
        increment = increment + alpha[:, None] * direction
        residual = residual - alpha[:, None] * image
        norm_next = squares(residual)
        direction = residual + (norm_next / norm_now)[:, None] * direction
        norm_now = norm_next
    return (increment, residual)


def solution(mesh):
    return jax.shard_map(
        shards,
        mesh=mesh,
        in_specs=(
            P(None, ("row", "col")),
            P(None, ("row", "col")),
            P(("row", "col")),
            P(("row", "col")),
            P(),
            P("row", "col", None, None),
        ),
        out_specs=(P(None, ("row", "col")), P(None, ("row", "col"))),
        check_vma=False,
    )
```

profile of v0, /device:TPU:0, one launch (start us, length us, event | category | flops | bytes accessed | tf_op | source)
XLA Modules:
  0.0 869.6 jit_solution(11168833523570514415)
XLA Ops:
  9.4 28.0 %all-gather.1 = f32[8,1,512]{2,1,0:T(1,128)S(1)} all-gather(f32[1,1,512]{2,1,0:T(1,128)S(1)} %bitcast.84), channel_id=1, replica_groups=mesh['row'=8,'col'=4] {'row'}, dimensions={0}, use_global_device_ids=true | all-gather | bytes 18432 | tf_op jit(solution)/shard_map/all_gather | solution.py:57
  37.4 5.2 all-gather
  42.6 7.5 all_gather.32
  50.0 7.5 all_gather.35
  58.2 95.6 %while.62 = (s32[]{:T(128)}, f32[2048]{0:T(1024)S(1)}, f32[4096]{0:T(1024)S(1)}, f32[8,512,512]{2,1,0:T(8,128)}, s32[8,3]{0,1:T(4,128)S(1)}, /*index=5*/f32[2048...) while((s32[]{:T(128)}, f32[2048]{0:T(1024)S(1)}, ...), condition=%wide.region_7.8_spmd, body=%wide.region_2.7_spmd.sunk | while | flops 204606480 | bytes 3716449 | solution.py:101
  61.6 2.6 multiply_add_fusion.6
  65.8 3.0 fusion.62
  73.5 2.6 multiply_add_fusion.6
  77.7 3.1 fusion.62
  85.6 2.6 multiply_add_fusion.6
  89.7 3.0 fusion.62
  97.5 2.6 multiply_add_fusion.6
  101.7 3.0 fusion.62
  109.4 2.6 multiply_add_fusion.6
  113.6 3.0 fusion.62
  121.4 2.6 multiply_add_fusion.6
  125.5 3.0 fusion.62
  133.3 2.6 multiply_add_fusion.6
  137.5 3.0 fusion.62
  145.3 2.6 multiply_add_fusion.6
  149.5 3.0 fusion.62
  154.0 50.7 %while.63 = (s32[]{:T(128)}, f32[64,2048]{1,0:T(8,128)S(1)}, f32[64,4096]{1,0:T(8,128)S(1)}, s32[8,3]{0,1:T(4,128)S(1)}, f32[64,4096]{1,0:T(8,128)}, /*index=5*/...) while((s32[]{:T(128)}, f32[64,2048]{1,0:T(8,128)S(1)}, ...), condition=%wide.region_11.12_spmd, body=%wide.region_10.11_spmd.sunk | while | flops 402718720 | bytes 2884853 | solution.py:151
  158.0 2.4 fusion.67
  164.3 2.4 fusion.67
  183.3 2.4 fusion.67
  208.7 35.5 %all-reduce.1 = f32[4096]{0:T(1024)S(1)} all-reduce(f32[4096]{0:T(1024)S(1)} %get-tuple-element.564), channel_id=3, replica_groups=mesh['row'=8,'col'=4] {'row'}, use_global_device_ids=true, to_apply=%region_9.10.clone | all-reduce | flops 4096 | bytes 32768
  244.2 6.1 all-reduce
  250.5 44.1 %reduce-scatter.9.cloned.1.call-done = f32[64,512]{1,0:T(8,128)} async-done(((f32[64,4096]{1,0:T(8,128)}), f32[64,512]{1,0:T(8,128)}) %reduce-scatter.9.cloned.1.call-update) | async-done | bytes 131088 | tf_op jit(solution)/shard_map/reduce_scatter | solution.py:155
  295.7 39.9 %all-reduce.2 = (f32[64]{0:T(128)S(1)}, f32[64]{0:T(128)S(1)}) all-reduce(f32[64]{0:T(128)S(1)} %get-tuple-element.575, f32[64]{0:T(128)S(1)} %get-tuple-element.574), channel_id=1, replica_groups=mesh['row'=8,'col'=4] {'row','col'}, use_global_device_ids=true, to_apply=%region_1.2 | all-reduce | flops 128 | bytes 1024 | tf_op jit(solution)/shard_map/psum | solution.py:46
  336.7 39.3 %psum.44 = f32[64]{0:T(128)S(1)} all-reduce(f32[64]{0:T(128)S(1)} %get-tuple-element.646), channel_id=1, replica_groups=mesh['row'=8,'col'=4] {'row','col'}, use_global_device_ids=true, to_apply=%region_17.18 | all-reduce | flops 64 | bytes 512 | tf_op jit(solution)/shard_map/psum | solution.py:46
  376.8 8.2 all_gather.37
  384.9 32.0 %all-gather.11.cloned.1.call-done = f32[64,4096]{1,0:T(8,128)} async-done(((f32[64,512]{1,0:T(8,128)}), f32[64,4096]{1,0:T(8,128)}) %all-gather.11.cloned.1.call-update) | async-done | bytes 1048592 | tf_op jit(solution)/shard_map/all_gather | solution.py:117
  417.0 51.1 %while.64 = (s32[]{:T(128)}, f32[64,2048]{1,0:T(8,128)S(1)}, f32[64,4096]{1,0:T(8,128)S(1)}, s32[8,3]{0,1:T(4,128)S(1)}, f32[64,4096]{1,0:T(8,128)}, /*index=5*/...) while((s32[]{:T(128)}, f32[64,2048]{1,0:T(8,128)S(1)}, ...), condition=%wide.region_19.20_spmd, body=%wide.region_18.19_spmd.sunk | while | flops 402718720 | bytes 2884853 | solution.py:151
  465.7 2.4 fusion.73
  469.7 19.7 %reduce-scatter.11.cloned.1.call-done = f32[64,512]{1,0:T(8,128)} async-done(((f32[64,2048]{1,0:T(8,128)}), f32[64,512]{1,0:T(8,128)}) %reduce-scatter.11.cloned.1.call-update) | async-done | bytes 131088 | tf_op jit(solution)/shard_map/reduce_scatter | solution.py:154
  489.4 68.0 %reduce-scatter.13.cloned.1.call-done = f32[64,512]{1,0:T(8,128)} async-done(((f32[64,4096]{1,0:T(8,128)}), f32[64,512]{1,0:T(8,128)}) %reduce-scatter.13.cloned.1.call-update) | async-done | bytes 131088 | tf_op jit(solution)/shard_map/reduce_scatter | solution.py:155
  558.6 39.9 %psum.45 = f32[64]{0:T(128)S(1)} all-reduce(f32[64]{0:T(128)S(1)} %multiply_reduce_fusion.4), channel_id=1, replica_groups=mesh['row'=8,'col'=4] {'row','col'}, use_global_device_ids=true, to_apply=%region_23.24 | all-reduce | flops 64 | bytes 512 | tf_op jit(solution)/shard_map/psum | solution.py:157
  599.6 39.3 %psum.46 = f32[64]{0:T(128)S(1)} all-reduce(f32[64]{0:T(128)S(1)} %get-tuple-element.644), channel_id=1, replica_groups=mesh['row'=8,'col'=4] {'row','col'}, use_global_device_ids=true, to_apply=%region_25.26 | all-reduce | flops 64 | bytes 512 | tf_op jit(solution)/shard_map/psum | solution.py:46
  639.7 8.3 all_gather.39
  648.1 31.8 %all-gather.13.cloned.1.call-done = f32[64,4096]{1,0:T(8,128)} async-done(((f32[64,512]{1,0:T(8,128)}), f32[64,4096]{1,0:T(8,128)}) %all-gather.13.cloned.1.call-update) | async-done | bytes 1048592 | tf_op jit(solution)/shard_map/all_gather | solution.py:117
  680.0 51.1 %while.65 = (s32[]{:T(128)}, f32[64,2048]{1,0:T(8,128)S(1)}, f32[64,4096]{1,0:T(8,128)S(1)}, s32[8,3]{0,1:T(4,128)S(1)}, f32[64,4096]{1,0:T(8,128)}, /*index=5*/...) while((s32[]{:T(128)}, f32[64,2048]{1,0:T(8,128)S(1)}, ...), condition=%wide.region_27.28_spmd, body=%wide.region_26.27_spmd.sunk | while | flops 402718720 | bytes 2884853 | solution.py:151
  684.0 2.4 fusion.79
  703.1 2.4 fusion.79
  722.3 2.4 fusion.79
  728.7 2.4 fusion.79
  732.5 19.9 %reduce-scatter.15.cloned.1.call-done = f32[64,512]{1,0:T(8,128)} async-done(((f32[64,2048]{1,0:T(8,128)}), f32[64,512]{1,0:T(8,128)}) %reduce-scatter.15.cloned.1.call-update) | async-done | bytes 131088 | tf_op jit(solution)/shard_map/reduce_scatter | solution.py:154
  752.4 67.6 %reduce-scatter.17.cloned.1.call-done = f32[64,512]{1,0:T(8,128)} async-done(((f32[64,4096]{1,0:T(8,128)}), f32[64,512]{1,0:T(8,128)}) %reduce-scatter.17.cloned.1.call-update) | async-done | bytes 131088 | tf_op jit(solution)/shard_map/reduce_scatter | solution.py:155
  821.1 39.9 %psum.47 = f32[64]{0:T(128)S(1)} all-reduce(f32[64]{0:T(128)S(1)} %multiply_reduce_fusion.2), channel_id=1, replica_groups=mesh['row'=8,'col'=4] {'row','col'}, use_global_device_ids=true, to_apply=%region_31.32 | all-reduce | flops 64 | bytes 512 | tf_op jit(solution)/shard_map/psum | solution.py:157
  (195 shorter events, 160.4 us)
Async XLA Ops:
  7.2 51.0 %all-gather.7.cloned.1.call-start = ((), (), s32[]{:S(2)}) async-start(), calls=%async_computation.6 | async-start | bytes 1179648 | tf_op jit(solution)/shard_map/all_gather | solution.py:56
  7.9 146.0 %all-gather.9.cloned.1.call-start = ((), (), s32[]{:S(2)}) async-start(), calls=%async_computation.7 | async-start | bytes 1179648 | tf_op jit(solution)/shard_map/all_gather | solution.py:117
  8.6 241.8 %reduce-scatter.7.cloned.1.call-start = ((), (), s32[]{:S(2)}) async-start(), calls=%async_computation.8 | async-start | bytes 655360 | tf_op jit(solution)/shard_map/reduce_scatter | solution.py:154
  153.9 52.3 %copy-start.11 = (u32[32]{0:T(128)S(1)}, u32[32]{0:T(128)}, u32[]{:S(2)}) copy-start(u32[32]{0:T(128)} %constant.217) | copy-start | bytes 388
  154.0 52.8 %copy-start.10 = (u32[32]{0:T(128)S(1)}, u32[32]{0:T(128)}, u32[]{:S(2)}) copy-start(u32[32]{0:T(128)} %constant.221) | copy-start | bytes 388
  154.0 96.4 %copy-start.9 = (f32[512]{0:T(512)S(1)}, f32[512]{0:T(512)}, u32[]{:S(2)}) copy-start(f32[512]{0:T(512)} %param.17) | copy-start | bytes 6148
  154.0 140.6 %copy-start.7 = (f32[64,512]{1,0:T(8,128)S(1)}, f32[64,512]{1,0:T(8,128)}, u32[]{:S(2)}) copy-start(f32[64,512]{1,0:T(8,128)} %param.14) | copy-start | bytes 393220
  204.7 0.8 copy-start.5
  204.8 1.2 copy-start.1
  205.6 89.0 %reduce-scatter.9.cloned.1.call-start = ((), (), s32[]{:S(2)}) async-start(), calls=%async_computation.9 | async-start | bytes 1179648 | tf_op jit(solution)/shard_map/reduce_scatter | solution.py:155
  206.1 210.8 %all-gather.11.cloned.1.call-start = ((), (), s32[]{:S(2)}) async-start(), calls=%async_computation.10 | async-start | bytes 1179648 | tf_op jit(solution)/shard_map/all_gather | solution.py:117
  376.7 112.7 %reduce-scatter.11.cloned.1.call-start = ((), (), s32[]{:S(2)}) async-start(), calls=%async_computation.11 | async-start | bytes 655360 | tf_op jit(solution)/shard_map/reduce_scatter | solution.py:154
  417.0 140.5 %copy-start.3 = (f32[64,512]{1,0:T(8,128)S(1)}, f32[64,512]{1,0:T(8,128)}, u32[]{:S(2)}) copy-start(f32[64,512]{1,0:T(8,128)} %multiply_add_fusion.4) | copy-start | bytes 393220
  468.1 0.8 copy-start.6
  468.1 1.2 copy-start.2
  468.9 88.5 %reduce-scatter.13.cloned.1.call-start = ((), (), s32[]{:S(2)}) async-start(), calls=%async_computation.12 | async-start | bytes 1179648 | tf_op jit(solution)/shard_map/reduce_scatter | solution.py:155
  469.7 210.2 %all-gather.13.cloned.1.call-start = ((), (), s32[]{:S(2)}) async-start(), calls=%async_computation.13 | async-start | bytes 1179648 | tf_op jit(solution)/shard_map/all_gather | solution.py:117
  639.7 112.8 %reduce-scatter.15.cloned.1.call-start = ((), (), s32[]{:S(2)}) async-start(), calls=%async_computation.14 | async-start | bytes 655360 | tf_op jit(solution)/shard_map/reduce_scatter | solution.py:154
  679.9 140.1 %copy-start.8 = (f32[64,512]{1,0:T(8,128)S(1)}, f32[64,512]{1,0:T(8,128)}, u32[]{:S(2)}) copy-start(f32[64,512]{1,0:T(8,128)} %multiply_add_fusion.3) | copy-start | bytes 393220
  731.1 0.8 copy-start.4
  731.1 1.2 copy-start
  731.9 88.1 %reduce-scatter.17.cloned.1.call-start = ((), (), s32[]{:S(2)}) async-start(), calls=%async_computation.15 | async-start | bytes 1179648 | tf_op jit(solution)/shard_map/reduce_scatter | solution.py:155
Sparse Core Ops, SparseCore 0:
  10.2 42.9 all-gather.6
  55.3 39.1 all-gather.8
  205.7 20.9 reduce-scatter.6
  230.0 64.5 reduce-scatter.8
  376.8 40.0 all-gather.10
  469.0 20.3 reduce-scatter.10
  492.8 64.5 reduce-scatter.12
  639.8 40.0 all-gather.12
  732.0 20.3 reduce-scatter.14
  755.7 64.3 reduce-scatter.16
where the time goes:
time: 873 us; the launch traced here: 870 us
  blocking collectives  304 us (35%)
  waiting for transfers between devices  285 us (33%)
  matrix products  130 us (15%)
  local copies, waits for them, and re-layouts  52 us (6%)
  loops' own time  41.7 us (5%)
  other arithmetic  40.3 us (5%)
  between operations  15.7 us (2%)
    reduce_scatter x3, waiting for transfers between devices, shards(): lax.psum_scatter(column_image, 'row', scatter_dimension=1, tiled=True)  180 us
    psum x3, blocking collectives, squares(): return lax.psum(jnp.sum(residual * residual, axis=1), ('row', 'col'))  118 us
    psum x2, blocking collectives, shards(): lax.psum(jnp.sum(direction * image, axis=1), ('row', 'col'))  79.8 us
    all_gather x3, waiting for transfers between devices, shards(): column_values = lax.all_gather(direction, 'row', axis=1, tiled=True)  63.8 us
    dot_general x24, matrix products, work(): lax.dot_general(take_segment(column_values, column_block), block_matrix,...  58.1 us
    dot_general x24, matrix products, work(): jnp.dot(take_segment(row_values, row_block), block_matrix, precision=lax....  47.4 us
    unnamed x2, blocking collectives  41.7 us
    reduce_scatter x3, waiting for transfers between devices, shards(): lax.psum_scatter(row_image, 'col', scatter_dimension=1, tiled=True)  39.6 us
  transfers between devices with their start and end apart: 10, of which 7 were waited for; matrix products, arithmetic and copies ran while one was open for 10% of the time, Pallas kernels for 0%

commit v1 on v0

v1 whole, which is shorter than its diff:
```python
import functools

import jax
import jax.numpy as jnp
from jax import lax
from jax.experimental import pallas as pl
from jax.experimental.pallas import tpu as pltpu
from jax.sharding import PartitionSpec as P

ITERS = 3
length_sq = 12.0
MESH = pl.DeviceIdType.MESH
VMEM = pl.BlockSpec(memory_space=pltpu.VMEM)
SMEM = pl.BlockSpec(memory_space=pltpu.SMEM)


def peers(rows, cols):
    r, c = lax.axis_index("row"), lax.axis_index("col")
    to_col = [(r, lax.rem(c + k, cols)) for k in range(1, cols)]
    to_row = [(lax.rem(r + k, rows), c) for k in range(1, rows)]
    from_col = [lax.rem(c + cols - k, cols) for k in range(1, cols)]
    from_row = [lax.rem(r + rows - k, rows) for k in range(1, rows)]
    return r, c, to_col, to_row, from_col, from_row


def greet(devices):
    barrier = pltpu.get_barrier_semaphore()
    for device in devices:
        pl.semaphore_signal(barrier, inc=1, device_id=device, device_id_type=MESH)
    pl.semaphore_wait(barrier, len(devices))


def remote(src, dst, send, recv, device):
    return pltpu.make_async_remote_copy(
        src_ref=src, dst_ref=dst, send_sem=send, recv_sem=recv,
        device_id=device, device_id_type=MESH,
    )


def gather_kernel(rows, cols, x, s, by_col, by_row, total, s1, s2, part,
                  send_c, recv_c, send_r, recv_r, send_1, recv_1, send_2, recv_2, own):
    r, c, to_col, to_row, from_col, from_row = peers(rows, cols)
    greet(to_col + to_row)
    small = [remote(s, s1.at[c], send_1.at[k], recv_1.at[k], d) for k, d in enumerate(to_col)]
    for copy in small:
        copy.start()
    bulk = [remote(x, by_row.at[r], send_r.at[k], recv_r.at[k], d) for k, d in enumerate(to_row)]
    bulk += [remote(x, by_col.at[c], send_c.at[k], recv_c.at[k], d) for k, d in enumerate(to_col)]
    for copy in bulk:
        copy.start()
    keep = [
        pltpu.make_async_copy(x, by_col.at[c], own.at[0]),
        pltpu.make_async_copy(x, by_row.at[r], own.at[1]),
        pltpu.make_async_copy(s, s1.at[c], own.at[2]),
    ]
    for copy in keep:
        copy.start()
    keep[2].wait()
    for k, q in enumerate(from_col):
        remote(s, s1.at[q], send_1.at[k], recv_1.at[k], to_col[k]).wait_recv()
    part[...] = jnp.sum(s1[...], axis=0)
    second = [remote(part, s2.at[r], send_2.at[k], recv_2.at[k], d) for k, d in enumerate(to_row)]
    for copy in second:
        copy.start()
    mine = pltpu.make_async_copy(part, s2.at[r], own.at[3])
    mine.start()
    for k, q in enumerate(from_row):
        remote(x, by_row.at[q], send_r.at[k], recv_r.at[k], to_row[k]).wait_recv()
    for k, q in enumerate(from_col):
        remote(x, by_col.at[q], send_c.at[k], recv_c.at[k], to_col[k]).wait_recv()
    for k, q in enumerate(from_row):
        remote(part, s2.at[q], send_2.at[k], recv_2.at[k], to_row[k]).wait_recv()
    mine.wait()
    keep[0].wait()
    keep[1].wait()
    total[...] = jnp.sum(s2[...], axis=0)
    for copy in small + bulk + second:
        copy.wait_send()


def scatter_kernel(rows, cols, by_col, by_row, s, out, total, got_c, got_r, s1, s2, part,
                   send_c, recv_c, send_r, recv_r, send_1, recv_1, send_2, recv_2, own):
    r, c, to_col, to_row, from_col, from_row = peers(rows, cols)
    greet(to_col + to_row)
    small = [remote(s, s1.at[c], send_1.at[k], recv_1.at[k], d) for k, d in enumerate(to_col)]
    for copy in small:
        copy.start()
    bulk = [remote(by_row.at[d[0]], got_r.at[k], send_r.at[k], recv_r.at[k], d)
            for k, d in enumerate(to_row)]
    bulk += [remote(by_col.at[d[1]], got_c.at[k], send_c.at[k], recv_c.at[k], d)
             for k, d in enumerate(to_col)]
    for copy in bulk:
        copy.start()
    keep = pltpu.make_async_copy(s, s1.at[c], own.at[0])
    keep.start()
    keep.wait()
    for k, q in enumerate(from_col):
        remote(s, s1.at[q], send_1.at[k], recv_1.at[k], to_col[k]).wait_recv()
    part[...] = jnp.sum(s1[...], axis=0)
    second = [remote(part, s2.at[r], send_2.at[k], recv_2.at[k], d) for k, d in enumerate(to_row)]
    for copy in second:
        copy.start()
    mine = pltpu.make_async_copy(part, s2.at[r], own.at[1])
    mine.start()
    for copy in bulk:
        copy.wait_recv()
    out[...] = (by_col[c] + by_row[r]) + (jnp.sum(got_c[...], axis=0) + jnp.sum(got_r[...], axis=0))
    for k, q in enumerate(from_row):
        remote(part, s2.at[q], send_2.at[k], recv_2.at[k], to_row[k]).wait_recv()
    mine.wait()
    total[...] = jnp.sum(s2[...], axis=0)
    for copy in small + bulk + second:
        copy.wait_send()


def semaphores(rows, cols):
    counts = [cols - 1, cols - 1, rows - 1, rows - 1, cols - 1, cols - 1, rows - 1, rows - 1, 4]
    return [pltpu.SemaphoreType.DMA((n,)) for n in counts]


def small_scratch(rows, cols):
    return [
        pltpu.VMEM((cols, 8, 128), jnp.float32),
        pltpu.VMEM((rows, 8, 128), jnp.float32),
        pltpu.VMEM((8, 128), jnp.float32),
    ]


def gather(x, s, rows, cols, number):
    f32 = jnp.float32
    return pl.pallas_call(
        functools.partial(gather_kernel, rows, cols),
        out_shape=(
            jax.ShapeDtypeStruct((cols,) + x.shape, f32),
            jax.ShapeDtypeStruct((rows,) + x.shape, f32),
            jax.ShapeDtypeStruct((8, 128), f32),
        ),
        in_specs=[VMEM] * 2,
        out_specs=(VMEM,) * 3,
        scratch_shapes=small_scratch(rows, cols) + semaphores(rows, cols),
        compiler_params=pltpu.CompilerParams(collective_id=number, has_side_effects=True),
    )(x, s)


def scatter(by_col, by_row, s, number):
    f32 = jnp.float32
    cols, rows = by_col.shape[0], by_row.shape[0]
    block = by_col.shape[1:]
    return pl.pallas_call(
        functools.partial(scatter_kernel, rows, cols),
        out_shape=(jax.ShapeDtypeStruct(block, f32), jax.ShapeDtypeStruct((8, 128), f32)),
        in_specs=[VMEM] * 3,
        out_specs=(VMEM,) * 2,
        scratch_shapes=[
            pltpu.VMEM((cols - 1,) + block, f32),
            pltpu.VMEM((rows - 1,) + block, f32),
        ] + small_scratch(rows, cols) + semaphores(rows, cols),
        compiler_params=pltpu.CompilerParams(collective_id=number, has_side_effects=True),
    )(by_col, by_row, s)


def build_kernel(slots, left, left_norm, left_label, right, right_norm, right_label,
                 coupling, high, low):
    number = pl.program_id(0)
    a, b = slots[number, 0], slots[number, 1]

    @pl.when(slots[number, 2] > 0)
    def _():
        products = jnp.dot(
            left[a], right[b], precision=lax.Precision.HIGHEST,
            preferred_element_type=jnp.float32,
        )
        ocean = right_label[b] > 0.5
        first = jnp.where(ocean, coupling[0, 1], coupling[0, 0])
        second = jnp.where(ocean, coupling[1, 1], coupling[1, 0])
        pair = jnp.where(left_label[a] > 0.5, second, first)
        tile = pair * jnp.exp(-(left_norm[a] + right_norm[b] - 2.0 * products) / length_sq)
        top = tile.astype(jnp.bfloat16)
        high[0] = top
        low[0] = (tile - top.astype(jnp.float32)).astype(jnp.bfloat16)


def build(slots, left, left_norm, left_label, right, right_norm, right_label, coupling):
    count, tile = slots.shape[0], left.shape[1]
    stored = jax.ShapeDtypeStruct((count, tile, tile), jnp.bfloat16)
    return pl.pallas_call(
        build_kernel,
        grid=(count,),
        out_shape=(stored, stored),
        in_specs=[SMEM] + [VMEM] * 6 + [SMEM],
        out_specs=(pl.BlockSpec((1, tile, tile), lambda i: (i, 0, 0)),) * 2,
    )(slots, left, left_norm, left_label, right, right_norm, right_label, coupling)


def times(values, high, low, side):
    dims = (((1,), (side,)), ((), ()))
    n = values.shape[0]
    top = values.astype(jnp.bfloat16).astype(jnp.float32)
    both = jnp.concatenate([top, values - top], axis=0).astype(jnp.bfloat16)
    wide = lax.dot_general(both, high, dims, preferred_element_type=jnp.float32)
    rest = lax.dot_general(
        top.astype(jnp.bfloat16), low, dims, preferred_element_type=jnp.float32
    )
    return wide[:n] + (wide[n:] + rest)


def fold(x):
    total = x[:, :128]
    for start in range(128, x.shape[1], 128):
        total = total + x[:, start:start + 128]
    return total


def sweep_kernel(rhs, slots, row_values, column_values, high, low, row_image, column_image, dots):
    number = pl.program_id(0)
    a, b = slots[number, 0], slots[number, 1]
    weigh = row_values.shape[1] > rhs

    @pl.when(number == 0)
    def _():
        row_image[...] = jnp.zeros_like(row_image)
        column_image[...] = jnp.zeros_like(column_image)
        dots[...] = jnp.zeros_like(dots)

    @pl.when(slots[number, 2] > 0)
    def _():
        rv, cv = row_values[a], column_values[b]
        t_high, t_low = high[0], low[0]
        right_part = times(cv, t_high, t_low, 1)
        left_part = times(rv, t_high, t_low, 0)
        row_image[a] += right_part
        column_image[b] += left_part
        rv, cv = rv[:rhs], cv[:rhs]
        amount = 2.0 * fold(right_part[:rhs] * rv)
        if weigh:
            amount = amount + fold(right_part[rhs:rhs + 1] * (rv * rv))
            amount = amount + fold(left_part[rhs:rhs + 1] * (cv * cv))
        dots[...] += amount


def sweep(rhs, slots, row_values, column_values, high, low):
    count, tile = high.shape[0], high.shape[1]
    whole = lambda shape: pl.BlockSpec(shape, lambda i: (0,) * len(shape))
    tiles = pl.BlockSpec((1, tile, tile), lambda i: (i, 0, 0))
    f32 = jnp.float32
    return pl.pallas_call(
        functools.partial(sweep_kernel, rhs),
        grid=(count,),
        out_shape=(
            jax.ShapeDtypeStruct(row_values.shape, f32),
            jax.ShapeDtypeStruct(column_values.shape, f32),
            jax.ShapeDtypeStruct((rhs, 128), f32),
        ),
        in_specs=[SMEM, VMEM, VMEM, tiles, tiles],
        out_specs=(whole(row_values.shape), whole(column_values.shape), whole((rhs, 128))),
    )(slots, row_values, column_values, high, low)


def spread(sums):
    return jnp.pad(sums[None, :], ((0, 7), (0, 128 - sums.shape[0])))


def shards(rows, cols, innovations, obs_factors, component, obs_error, coupling, tile_slots):
    slots = tile_slots[0, 0]
    rhs, tile = innovations.shape
    depth = obs_factors.shape[0]
    labels = jnp.pad(component.astype(jnp.float32)[None, :], ((0, 7), (0, 0)))
    packed = jnp.concatenate([obs_factors, labels, innovations], axis=0)
    by_col, by_row, total = gather(
        packed, spread(jnp.sum(innovations * innovations, axis=1)), rows, cols, 0
    )
    norm_now = total[0, :rhs]

    left = by_col[:, :depth]
    right = by_row[:, :depth]
    high, low = build(
        slots,
        jnp.swapaxes(left, 1, 2),
        jnp.sum(left * left, axis=1)[:, :, None],
        by_col[:, depth][:, :, None],
        right,
        jnp.sum(right * right, axis=1)[:, None, :],
        by_row[:, depth][:, None, :],
        coupling,
    )

    row_values = by_col[:, depth + 8:]
    column_values = by_row[:, depth + 8:]

    def with_ones(values):
        ones = jnp.ones((values.shape[0], 1, tile), jnp.float32)
        rest = jnp.zeros((values.shape[0], 15, tile), jnp.float32)
        return jnp.concatenate([values, ones, rest], axis=1)

    increment = jnp.zeros_like(innovations)
    residual = innovations
    direction = innovations
    diagonal = None
    for repeat in range(ITERS):
        if repeat == 0:
            row_image, column_image, dots = sweep(
                rhs, slots, with_ones(row_values), with_ones(column_values), high, low
            )
            row_image, column_image = row_image[:, :rhs + 8], column_image[:, :rhs + 8]
            own = obs_error
        else:
            row_image, column_image, dots = sweep(
                rhs, slots, row_values, column_values, high, low
            )
            own = diagonal
        part = jnp.sum(dots, axis=1) + jnp.sum(own[None, :] * direction * direction, axis=1)
        product, total = scatter(row_image, column_image, spread(part), 1 if repeat == 0 else 2)
        if repeat == 0:
            diagonal = obs_error + product[rhs]
        image = diagonal[None, :] * direction + product[:rhs]
        alpha = norm_now / total[0, :rhs]
        increment = increment + alpha[:, None] * direction
        residual = residual - alpha[:, None] * image
        if repeat + 1 < ITERS:
            by_col, by_row, total = gather(
                residual, spread(jnp.sum(residual * residual, axis=1)), rows, cols, 3
            )
            norm_next = total[0, :rhs]
            beta = (norm_next / norm_now)[:, None]
            direction = residual + beta * direction
            row_values = by_col + beta * row_values
            column_values = by_row + beta * column_values
            norm_now = norm_next
    return (increment, residual)


def solution(mesh):
    return jax.shard_map(
        functools.partial(shards, mesh.shape["row"], mesh.shape["col"]),
        mesh=mesh,
        in_specs=(
            P(None, ("row", "col")),
            P(None, ("row", "col")),
            P(("row", "col")),
            P(("row", "col")),
            P(),
            P("row", "col", None, None),
        ),
        out_specs=(P(None, ("row", "col")), P(None, ("row", "col"))),
        check_vma=False,
    )
```

time: 873 us -> 300 us (0.34)
  blocking collectives: 304 us -> 0 us
  waiting for transfers between devices: 285 us -> 0 us
  Pallas kernels: 0 us -> 251 us
  matrix products: 130 us -> 0 us
  loops' own time: 41.7 us -> 0 us
  local copies, waits for them, and re-layouts: 52 us -> 15.2 us
  between operations: 15.7 us -> 0.82 us
  other arithmetic: 40.3 us -> 31 us
    pallas_call x0 -> x10, Pallas kernels: none -> 251 us  [the longest x3 118 us: gather(): pl.pallas_call(functools.partial(gather_kernel, rows, cols), out_shape=(j...]
    reduce_scatter x6 -> x0, waiting for transfers between devices: 219 us -> none  [the longest x3 180 us: shards(): lax.psum_scatter(column_image, 'row', scatter_dimension=1, tiled=True)]
    psum x5 -> x0, blocking collectives: 198 us -> none  [the longest x3 118 us: squares(): return lax.psum(jnp.sum(residual * residual, axis=1), ('row', 'col'))]
    dot_general x56 -> x0, matrix products: 130 us -> none  [the longest x24 58.1 us: work(): lax.dot_general(take_segment(column_values, column_block), block_matrix,...]
    all_gather x6 -> x0, blocking collectives: 64.6 us -> none  [the longest x1 28 us: shards(): lax.all_gather(labels_float, 'row', axis=0, tiled=True)]
    all_gather x4 -> x0, waiting for transfers between devices: 63.8 us -> none  [the longest x3 63.8 us: shards(): column_values = lax.all_gather(direction, 'row', axis=1, tiled=True)]
    unnamed x2 -> x0, blocking collectives: 41.7 us -> none
    another operation x4 -> x0, loops' own time: 41.7 us -> none  [the longest x3 31.8 us: shards(): row_image, column_image = lax.fori_loop(0, count, sweep, start_image)]
  transfers between devices with their start and end apart: 10 -> 0, of which waited for: 7 -> 0; matrix products, arithmetic and copies ran while one was open for 10% -> 0% of each run, Pallas kernels for 0% -> 0%
where the time goes in v1:
time: 300 us; the launch traced here: 298 us
  Pallas kernels  251 us (84%)
  other arithmetic  31 us (10%)
  local copies, waits for them, and re-layouts  15.2 us (5%)
    pallas_call x3, Pallas kernels, gather(): pl.pallas_call(functools.partial(gather_kernel, rows, cols), out_shape=(j...  118 us
    pallas_call x3, Pallas kernels, scatter(): pl.pallas_call(functools.partial(scatter_kernel, rows, cols), out_shape=(...  99.1 us
    pallas_call x3, Pallas kernels, sweep(): pl.pallas_call(functools.partial(sweep_kernel, rhs), grid=(count,), out_s...  25.4 us
    pallas_call x1, Pallas kernels, build(): pl.pallas_call(build_kernel, grid=(count,), out_shape=(stored, stored), i...  9.32 us

profile of v1, /device:TPU:0, one launch (start us, length us, event | category | flops | bytes accessed | tf_op | source)
XLA Modules:
  0.0 298.4 jit_solution(3830265761614585894)
XLA Ops:
  0.6 1.0 fusion.8
  1.7 0.6 pad.24.s
  2.3 0.7 convert_element_type.12
  3.0 1.7 fusion.x
  4.6 59.0 %shard_map.77 = (f32[4,136,512]{2,1,0:T(8,128)}, f32[8,136,512]{2,1,0:T(8,128)}, f32[8,128]{1,0:T(8,128)}) custom-call(f32[136,512]{1,0:T(8,128)} %fusion.x, f32[8,128]{1,0:T(8,128)} %pad.24.s), custom_call_target="tpu_custom_call" | custom-call | tf_op jit(solution)/shard_map/pallas_call | solution.py:131
  63.7 1.8 copy.14
  65.4 1.2 multiply_reduce_fusion.1
  66.6 1.4 copy.16.left_norm
  68.1 3.0 multiply_reduce_fusion
  71.0 0.6 broadcast_in_dim.54.right_norm
  71.7 1.3 broadcast_in_dim_squeeze.4.left_label
  73.0 1.5 slice.54.right_label
  74.5 0.7 copy.21
  75.2 9.3 %shard_map.78 = (bf16[8,512,512]{2,1,0:T(8,128)(2,1)}, bf16[8,512,512]{2,1,0:T(8,128)(2,1)}) custom-call(s32[8,3]{1,0:T(8,128)} %bitcast.27, f32[4,512,64]{2,1,0:T(8,128)} %get-tuple-element.66.left, f32[4,512,1]{2,1,0:T(8,128)} %copy.16.left_norm, f32[4,512,1]{2,1,0:T(8,128)} %broadcast_in_dim_squeeze.4.left_label, f32[8,64,512]{2,1,0:T(8,128)} %get-tuple-element.63.right, ...), custom_call_target="tpu_custom_call" | custom-call | tf_op jit(solution)/shard_map/pallas_call | solution.py:186
  84.7 1.3 maximum_maximum_fusion.column_values
  86.1 1.0 maximum_maximum_fusion.1.row_values
  87.1 8.7 %shard_map.79 = (f32[4,80,512]{2,1,0:T(8,128)}, f32[8,80,512]{2,1,0:T(8,128)}, f32[64,128]{1,0:T(8,128)}) custom-call(s32[8,3]{1,0:T(8,128)} %bitcast.28, f32[4,80,512]{2,1,0:T(8,128)} %maximum_maximum_fusion.1.row_values, f32[8,80,512]{2,1,0:T(8,128)} %maximum_maximum_fusion.column_values, bf16[8,512,512]{2,1,0:T(8,128)(2,1)} %get-tuple-element.31.high, ...), custom_call_target="tpu_custom_call" | custom-call | tf_op jit(solution)/shard_map/pallas_call | solution.py:246
  95.7 0.9 reduce_sum.102
  96.7 0.6 pad.25.s
  97.3 2.4 slice.56.by_row
  99.7 0.9 slice.55.by_col
  100.6 37.8 %shard_map.80 = (f32[72,512]{1,0:T(8,128)}, f32[8,128]{1,0:T(8,128)}) custom-call(f32[4,72,512]{2,1,0:T(8,128)} %slice.55.by_col, f32[8,72,512]{2,1,0:T(8,128)} %slice.56.by_row, f32[8,128]{1,0:T(8,128)} %pad.25.s), custom_call_target="tpu_custom_call" | custom-call | tf_op jit(solution)/shard_map/pallas_call | solution.py:149
  138.4 0.7 fusion.9
  139.1 0.7 slice.58
  139.8 1.7 multiply_reduce_fusion.3
  141.6 0.6 pad.26.s
  142.2 29.5 %shard_map.81 = (f32[4,64,512]{2,1,0:T(8,128)}, f32[8,64,512]{2,1,0:T(8,128)}, f32[8,128]{1,0:T(8,128)}) custom-call(f32[64,512]{1,0:T(8,128)} %get-tuple-element.61.x, f32[8,128]{1,0:T(8,128)} %pad.26.s), custom_call_target="tpu_custom_call" | custom-call | tf_op jit(solution)/shard_map/pallas_call | solution.py:131
  171.7 0.7 divide_bitcast_fusion.1
  172.4 1.1 fusion.2
  173.5 2.9 multiply_add_fusion.1.column_values
  176.4 0.9 multiply_add_fusion.3.row_values
  177.3 8.4 %shard_map.82 = (f32[4,64,512]{2,1,0:T(8,128)}, f32[8,64,512]{2,1,0:T(8,128)}, f32[64,128]{1,0:T(8,128)}) custom-call(s32[8,3]{1,0:T(8,128)} %bitcast.29, f32[4,64,512]{2,1,0:T(8,128)} %multiply_add_fusion.3.row_values, f32[8,64,512]{2,1,0:T(8,128)} %multiply_add_fusion.1.column_values, bf16[8,512,512]{2,1,0:T(8,128)(2,1)} %get-tuple-element.31.high, ...), custom_call_target="tpu_custom_call" | custom-call | tf_op jit(solution)/shard_map/pallas_call | solution.py:246
  185.7 1.0 reduce_sum.105
  187.3 30.4 %shard_map.83 = (f32[64,512]{1,0:T(8,128)}, f32[8,128]{1,0:T(8,128)}) custom-call(f32[4,64,512]{2,1,0:T(8,128)} %get-tuple-element.41.by_col, f32[8,64,512]{2,1,0:T(8,128)} %get-tuple-element.42.by_row, f32[8,128]{1,0:T(8,128)} %pad.27.s), custom_call_target="tpu_custom_call" | custom-call | tf_op jit(solution)/shard_map/pallas_call | solution.py:149
  217.7 0.7 fusion.10
  218.4 1.7 multiply_reduce_fusion.2
  220.2 0.6 pad.28.s
  220.8 29.0 %shard_map.84 = (f32[4,64,512]{2,1,0:T(8,128)}, f32[8,64,512]{2,1,0:T(8,128)}, f32[8,128]{1,0:T(8,128)}) custom-call(f32[64,512]{1,0:T(8,128)} %get-tuple-element.57.x, f32[8,128]{1,0:T(8,128)} %pad.28.s), custom_call_target="tpu_custom_call" | custom-call | tf_op jit(solution)/shard_map/pallas_call | solution.py:131
  249.8 0.7 divide_bitcast_fusion
  250.5 1.1 fusion.5
  251.6 2.7 multiply_add_fusion.column_values
  254.3 0.9 multiply_add_fusion.2.row_values
  255.2 8.4 %shard_map.85 = (f32[4,64,512]{2,1,0:T(8,128)}, f32[8,64,512]{2,1,0:T(8,128)}, f32[64,128]{1,0:T(8,128)}) custom-call(s32[8,3]{1,0:T(8,128)} %bitcast.30, f32[4,64,512]{2,1,0:T(8,128)} %multiply_add_fusion.2.row_values, f32[8,64,512]{2,1,0:T(8,128)} %multiply_add_fusion.column_values, bf16[8,512,512]{2,1,0:T(8,128)(2,1)} %get-tuple-element.31.high, ...), custom_call_target="tpu_custom_call" | custom-call | tf_op jit(solution)/shard_map/pallas_call | solution.py:246
  263.6 0.9 reduce_sum.108
  264.5 0.6 pad.29.s
  265.1 30.8 %shard_map.86 = (f32[64,512]{1,0:T(8,128)}, f32[8,128]{1,0:T(8,128)}) custom-call(f32[4,64,512]{2,1,0:T(8,128)} %get-tuple-element.49.by_col, f32[8,64,512]{2,1,0:T(8,128)} %get-tuple-element.50.by_row, f32[8,128]{1,0:T(8,128)} %pad.29.s), custom_call_target="tpu_custom_call" | custom-call | tf_op jit(solution)/shard_map/pallas_call | solution.py:149
  295.9 0.7 fusion.11
  296.6 1.7 fusion.7
  (32 shorter events, 0.9 us)
Async XLA Ops:
  68.1 3.6 %copy-start.2 = (f32[4,136,512]{2,1,0:T(8,128)S(1)}, f32[4,136,512]{2,1,0:T(8,128)}, u32[]{:S(2)}) copy-start(f32[4,136,512]{2,1,0:T(8,128)} %get-tuple-element.29) | copy-start | bytes 3342340
  68.1 6.5 %copy-start.10 = (s32[1,1,8,3]{2,1,3,0:T(1,128)S(1)}, s32[1,1,8,3]{2,1,3,0:T(1,128)}, u32[]{:S(2)}) copy-start(s32[1,1,8,3]{2,1,3,0:T(1,128)} %param.11) | copy-start | bytes 292
  95.7 4.0 %copy-start.6 = (f32[4,80,512]{2,1,0:T(8,128)S(1)}, f32[4,80,512]{2,1,0:T(8,128)}, u32[]{:S(2)}) copy-start(f32[4,80,512]{2,1,0:T(8,128)} %get-tuple-element.33) | copy-start | bytes 1966084
  99.7 40.1 %copy-start.9 = (f32[512]{0:T(512)S(1)}, f32[512]{0:T(512)}, u32[]{:S(2)}) copy-start(f32[512]{0:T(512)} %param.9) | copy-start | bytes 6148
  99.7 40.2 %copy-start.3 = (f32[64,512]{1,0:T(8,128)S(1)}, f32[64,512]{1,0:T(8,128)}, u32[]{:S(2)}) copy-start(f32[64,512]{1,0:T(8,128)} %param.6) | copy-start | bytes 393220
  173.5 2.9 copy-start.7
  185.7 32.7 %copy-start.4 = (f32[64,512]{1,0:T(8,128)S(1)}, f32[64,512]{1,0:T(8,128)}, u32[]{:S(2)}) copy-start(f32[64,512]{1,0:T(8,128)} %get-tuple-element.61.x) | copy-start | bytes 393220
  185.7 65.9 %copy-start = (f32[8,64,512]{2,1,0:T(8,128)S(1)}, f32[8,64,512]{2,1,0:T(8,128)}, u32[]{:S(2)}) copy-start(f32[8,64,512]{2,1,0:T(8,128)} %multiply_add_fusion.1.column_values) | copy-start | bytes 3145732
  251.6 2.7 copy-start.1
  251.6 2.7 copy-start.8
  263.6 33.0 %copy-start.5 = (f32[64,512]{1,0:T(8,128)S(1)}, f32[64,512]{1,0:T(8,128)}, u32[]{:S(2)}) copy-start(f32[64,512]{1,0:T(8,128)} %get-tuple-element.57.x) | copy-start | bytes 393220

commit v2 on v1

--- a/solution.py
+++ b/solution.py
@@ -37,14 +37,36 @@
     )
 
 
+def legs(rows):
+    outer = 4 if rows % 4 == 0 else rows
+    order = sorted(range(1, outer), key=lambda k: (abs(2 * k - outer), k))
+    return outer, rows // outer, order
+
+
 def gather_kernel(rows, cols, x, s, by_col, by_row, total, s1, s2, part,
-                  send_c, recv_c, send_r, recv_r, send_1, recv_1, send_2, recv_2, own):
+                  send_c, recv_c, send_z, recv_z, send_x, recv_x,
+                  send_1, recv_1, send_2, recv_2, own):
     r, c, to_col, to_row, from_col, from_row = peers(rows, cols)
+    outer, inner, order = legs(rows)
+    z, w = lax.div(r, inner), lax.rem(r, inner)
     greet(to_col + to_row)
     small = [remote(s, s1.at[c], send_1.at[k], recv_1.at[k], d) for k, d in enumerate(to_col)]
     for copy in small:
         copy.start()
-    bulk = [remote(x, by_row.at[r], send_r.at[k], recv_r.at[k], d) for k, d in enumerate(to_row)]
+    to_z = {k: (lax.rem(z + k, outer) * inner + w, c) for k in order}
+    to_x = {j: (z * inner + lax.rem(w + j, inner), c) for j in range(1, inner)}
+    from_z = {k: lax.rem(z + outer - k, outer) for k in [0] + order}
+    from_x = {j: lax.rem(w + inner - j, inner) for j in range(1, inner)}
+
+    def along(k, slot):
+        return remote(x, by_row.at[slot], send_z.at[k - 1], recv_z.at[k - 1], to_z[k])
+
+    def across(k, j, slot):
+        source = x if k == 0 else by_row.at[slot]
+        return remote(source, by_row.at[slot], send_x.at[k, j - 1], recv_x.at[k, j - 1], to_x[j])
+
+    bulk = [along(k, r) for k in order]
+    bulk += [across(0, j, r) for j in to_x]
     bulk += [remote(x, by_col.at[c], send_c.at[k], recv_c.at[k], d) for k, d in enumerate(to_col)]
     for copy in bulk:
         copy.start()
@@ -64,10 +86,18 @@
         copy.start()
     mine = pltpu.make_async_copy(part, s2.at[r], own.at[3])
     mine.start()
-    for k, q in enumerate(from_row):
-        remote(x, by_row.at[q], send_r.at[k], recv_r.at[k], to_row[k]).wait_recv()
+    for k in order:
+        slot = from_z[k] * inner + w
+        along(k, slot).wait_recv()
+        for j in to_x:
+            copy = across(k, j, slot)
+            copy.start()
+            bulk.append(copy)
     for k, q in enumerate(from_col):
         remote(x, by_col.at[q], send_c.at[k], recv_c.at[k], to_col[k]).wait_recv()
+    for k in [0] + order:
+        for j in to_x:
+            across(k, j, from_z[k] * inner + from_x[j]).wait_recv()
     for k, q in enumerate(from_row):
         remote(part, s2.at[q], send_2.at[k], recv_2.at[k], to_row[k]).wait_recv()
     mine.wait()
@@ -78,18 +108,28 @@
         copy.wait_send()
 
 
-def scatter_kernel(rows, cols, by_col, by_row, s, out, total, got_c, got_r, s1, s2, part,
-                   send_c, recv_c, send_r, recv_r, send_1, recv_1, send_2, recv_2, own):
+def scatter_kernel(rows, cols, by_col, by_row, s, out, total, got_c, got_z, got_x, stage,
+                   s1, s2, part, send_c, recv_c, send_z, recv_z, send_x, recv_x,
+                   send_1, recv_1, send_2, recv_2, own):
     r, c, to_col, to_row, from_col, from_row = peers(rows, cols)
+    outer, inner, order = legs(rows)
+    z, w = lax.div(r, inner), lax.rem(r, inner)
     greet(to_col + to_row)
     small = [remote(s, s1.at[c], send_1.at[k], recv_1.at[k], d) for k, d in enumerate(to_col)]
     for copy in small:
         copy.start()
-    bulk = [remote(by_row.at[d[0]], got_r.at[k], send_r.at[k], recv_r.at[k], d)
-            for k, d in enumerate(to_row)]
-    bulk += [remote(by_col.at[d[1]], got_c.at[k], send_c.at[k], recv_c.at[k], d)
-             for k, d in enumerate(to_col)]
-    for copy in bulk:
+    across = {}
+    for k in order + [0]:
+        for j in range(1, inner):
+            side = lax.rem(w + j, inner)
+            across[k, j] = remote(
+                by_row.at[lax.rem(z + k, outer) * inner + side], got_x.at[k, j - 1],
+                send_x.at[k, j - 1], recv_x.at[k, j - 1], (z * inner + side, c),
+            )
+            across[k, j].start()
+    flat = [remote(by_col.at[d[1]], got_c.at[k], send_c.at[k], recv_c.at[k], d)
+            for k, d in enumerate(to_col)]
+    for copy in flat:
         copy.start()
     keep = pltpu.make_async_copy(s, s1.at[c], own.at[0])
     keep.start()
@@ -102,20 +142,41 @@
         copy.start()
     mine = pltpu.make_async_copy(part, s2.at[r], own.at[1])
     mine.start()
-    for copy in bulk:
+
+    def joined(k):
+        value = by_row[lax.rem(z + k, outer) * inner + w]
+        for j in range(1, inner):
+            across[k, j].wait_recv()
+            value = value + got_x[k, j - 1]
+        return value
+
+    along = []
+    for k in order:
+        stage[k - 1] = joined(k)
+        copy = remote(stage.at[k - 1], got_z.at[k - 1], send_z.at[k - 1], recv_z.at[k - 1],
+                      (lax.rem(z + k, outer) * inner + w, c))
+        copy.start()
+        along.append(copy)
+    for copy in flat:
         copy.wait_recv()
-    out[...] = (by_col[c] + by_row[r]) + (jnp.sum(got_c[...], axis=0) + jnp.sum(got_r[...], axis=0))
+    out[...] = joined(0) + (by_col[c] + jnp.sum(got_c[...], axis=0))
+    for copy in along:
+        copy.wait_recv()
+    out[...] += jnp.sum(got_z[...], axis=0)
     for k, q in enumerate(from_row):
         remote(part, s2.at[q], send_2.at[k], recv_2.at[k], to_row[k]).wait_recv()
     mine.wait()
     total[...] = jnp.sum(s2[...], axis=0)
-    for copy in small + bulk + second:
+    for copy in small + flat + along + second + list(across.values()):
         copy.wait_send()
 
 
 def semaphores(rows, cols):
-    counts = [cols - 1, cols - 1, rows - 1, rows - 1, cols - 1, cols - 1, rows - 1, rows - 1, 4]
-    return [pltpu.SemaphoreType.DMA((n,)) for n in counts]
+    outer, inner, order = legs(rows)
+    sides = (outer, max(inner - 1, 1))
+    shapes = [(cols - 1,)] * 2 + [(outer - 1,)] * 2 + [sides] * 2
+    shapes += [(cols - 1,)] * 2 + [(rows - 1,)] * 2 + [(4,)]
+    return [pltpu.SemaphoreType.DMA(shape) for shape in shapes]
 
 
 def small_scratch(rows, cols):
@@ -146,6 +207,7 @@
     f32 = jnp.float32
     cols, rows = by_col.shape[0], by_row.shape[0]
     block = by_col.shape[1:]
+    outer, inner, order = legs(rows)
     return pl.pallas_call(
         functools.partial(scatter_kernel, rows, cols),
         out_shape=(jax.ShapeDtypeStruct(block, f32), jax.ShapeDtypeStruct((8, 128), f32)),
@@ -153,43 +215,48 @@
         out_specs=(VMEM,) * 2,
         scratch_shapes=[
             pltpu.VMEM((cols - 1,) + block, f32),
-            pltpu.VMEM((rows - 1,) + block, f32),
+            pltpu.VMEM((outer - 1,) + block, f32),
+            pltpu.VMEM((outer, max(inner - 1, 1)) + block, f32),
+            pltpu.VMEM((outer - 1,) + block, f32),
         ] + small_scratch(rows, cols) + semaphores(rows, cols),
         compiler_params=pltpu.CompilerParams(collective_id=number, has_side_effects=True),
     )(by_col, by_row, s)
 
 
-def build_kernel(slots, left, left_norm, left_label, right, right_norm, right_label,
-                 coupling, high, low):
+def build_kernel(depth, slots, by_col, by_row, coupling, high, low):
     number = pl.program_id(0)
     a, b = slots[number, 0], slots[number, 1]
 
     @pl.when(slots[number, 2] > 0)
     def _():
+        left = jnp.transpose(by_col[a, :depth + 8])
+        left, left_label = left[:, :depth], left[:, depth:depth + 1]
+        right, right_label = by_row[b, :depth], by_row[b, depth:depth + 1]
+        left_norm = jnp.sum(left * left, axis=1, keepdims=True)
+        right_norm = jnp.sum(right * right, axis=0, keepdims=True)
         products = jnp.dot(
-            left[a], right[b], precision=lax.Precision.HIGHEST,
-            preferred_element_type=jnp.float32,
+            left, right, precision=lax.Precision.HIGHEST, preferred_element_type=jnp.float32
         )
-        ocean = right_label[b] > 0.5
+        ocean = right_label > 0.5
         first = jnp.where(ocean, coupling[0, 1], coupling[0, 0])
         second = jnp.where(ocean, coupling[1, 1], coupling[1, 0])
-        pair = jnp.where(left_label[a] > 0.5, second, first)
-        tile = pair * jnp.exp(-(left_norm[a] + right_norm[b] - 2.0 * products) / length_sq)
+        pair = jnp.where(left_label > 0.5, second, first)
+        tile = pair * jnp.exp(-(left_norm + right_norm - 2.0 * products) / length_sq)
         top = tile.astype(jnp.bfloat16)
         high[0] = top
         low[0] = (tile - top.astype(jnp.float32)).astype(jnp.bfloat16)
 
 
-def build(slots, left, left_norm, left_label, right, right_norm, right_label, coupling):
-    count, tile = slots.shape[0], left.shape[1]
+def build(depth, slots, by_col, by_row, coupling):
+    count, tile = slots.shape[0], by_col.shape[2]
     stored = jax.ShapeDtypeStruct((count, tile, tile), jnp.bfloat16)
     return pl.pallas_call(
-        build_kernel,
+        functools.partial(build_kernel, depth),
         grid=(count,),
         out_shape=(stored, stored),
-        in_specs=[SMEM] + [VMEM] * 6 + [SMEM],
+        in_specs=[SMEM, VMEM, VMEM, SMEM],
         out_specs=(pl.BlockSpec((1, tile, tile), lambda i: (i, 0, 0)),) * 2,
-    )(slots, left, left_norm, left_label, right, right_norm, right_label, coupling)
+    )(slots, by_col, by_row, coupling)
 
 
 def times(values, high, low, side):
@@ -211,10 +278,12 @@
     return total
 
 
-def sweep_kernel(rhs, slots, row_values, column_values, high, low, row_image, column_image, dots):
+def sweep_kernel(rhs, start, slots, row_values, column_values, high, low,
+                 row_image, column_image, dots):
     number = pl.program_id(0)
     a, b = slots[number, 0], slots[number, 1]
-    weigh = row_values.shape[1] > rhs
+    kept = row_image.shape[1]
+    weigh = kept > rhs
 
     @pl.when(number == 0)
     def _():
@@ -224,13 +293,17 @@
 
     @pl.when(slots[number, 2] > 0)
     def _():
-        rv, cv = row_values[a], column_values[b]
+        rv, cv = row_values[a, start:start + rhs], column_values[b, start:start + rhs]
         t_high, t_low = high[0], low[0]
-        right_part = times(cv, t_high, t_low, 1)
-        left_part = times(rv, t_high, t_low, 0)
-        row_image[a] += right_part
-        column_image[b] += left_part
-        rv, cv = rv[:rhs], cv[:rhs]
+        rows, columns = rv, cv
+        if weigh:
+            ones = jnp.ones((16, rv.shape[1]), jnp.float32)
+            rows = jnp.concatenate([rv, ones], axis=0)
+            columns = jnp.concatenate([cv, ones], axis=0)
+        right_part = times(columns, t_high, t_low, 1)
+        left_part = times(rows, t_high, t_low, 0)
+        row_image[a] += right_part[:kept]
+        column_image[b] += left_part[:kept]
         amount = 2.0 * fold(right_part[:rhs] * rv)
         if weigh:
             amount = amount + fold(right_part[rhs:rhs + 1] * (rv * rv))
@@ -238,21 +311,19 @@
         dots[...] += amount
 
 
-def sweep(rhs, slots, row_values, column_values, high, low):
+def sweep(rhs, start, kept, slots, row_values, column_values, high, low):
     count, tile = high.shape[0], high.shape[1]
     whole = lambda shape: pl.BlockSpec(shape, lambda i: (0,) * len(shape))
     tiles = pl.BlockSpec((1, tile, tile), lambda i: (i, 0, 0))
-    f32 = jnp.float32
+    shapes = (
+        (row_values.shape[0], kept, tile), (column_values.shape[0], kept, tile), (rhs, 128)
+    )
     return pl.pallas_call(
-        functools.partial(sweep_kernel, rhs),
+        functools.partial(sweep_kernel, rhs, start),
         grid=(count,),
-        out_shape=(
-            jax.ShapeDtypeStruct(row_values.shape, f32),
-            jax.ShapeDtypeStruct(column_values.shape, f32),
-            jax.ShapeDtypeStruct((rhs, 128), f32),
-        ),
+        out_shape=tuple(jax.ShapeDtypeStruct(shape, jnp.float32) for shape in shapes),
         in_specs=[SMEM, VMEM, VMEM, tiles, tiles],
-        out_specs=(whole(row_values.shape), whole(column_values.shape), whole((rhs, 128))),
+        out_specs=tuple(whole(shape) for shape in shapes),
     )(slots, row_values, column_values, high, low)
 
 
@@ -262,7 +333,7 @@
 
 def shards(rows, cols, innovations, obs_factors, component, obs_error, coupling, tile_slots):
     slots = tile_slots[0, 0]
-    rhs, tile = innovations.shape
+    rhs = innovations.shape[0]
     depth = obs_factors.shape[0]
     labels = jnp.pad(component.astype(jnp.float32)[None, :], ((0, 7), (0, 0)))
     packed = jnp.concatenate([obs_factors, labels, innovations], axis=0)
@@ -271,26 +342,9 @@
     )
     norm_now = total[0, :rhs]
 
-    left = by_col[:, :depth]
-    right = by_row[:, :depth]
-    high, low = build(
-        slots,
-        jnp.swapaxes(left, 1, 2),
-        jnp.sum(left * left, axis=1)[:, :, None],
-        by_col[:, depth][:, :, None],
-        right,
-        jnp.sum(right * right, axis=1)[:, None, :],
-        by_row[:, depth][:, None, :],
-        coupling,
-    )
-
+    high, low = build(depth, slots, by_col, by_row, coupling)
     row_values = by_col[:, depth + 8:]
     column_values = by_row[:, depth + 8:]
-
-    def with_ones(values):
-        ones = jnp.ones((values.shape[0], 1, tile), jnp.float32)
-        rest = jnp.zeros((values.shape[0], 15, tile), jnp.float32)
-        return jnp.concatenate([values, ones, rest], axis=1)
 
     increment = jnp.zeros_like(innovations)
     residual = innovations
@@ -299,13 +353,12 @@
     for repeat in range(ITERS):
         if repeat == 0:
             row_image, column_image, dots = sweep(
-                rhs, slots, with_ones(row_values), with_ones(column_values), high, low
+                rhs, depth + 8, rhs + 8, slots, by_col, by_row, high, low
             )
-            row_image, column_image = row_image[:, :rhs + 8], column_image[:, :rhs + 8]
             own = obs_error
         else:
             row_image, column_image, dots = sweep(
-                rhs, slots, row_values, column_values, high, low
+                rhs, 0, rhs, slots, row_values, column_values, high, low
             )
             own = diagonal
         part = jnp.sum(dots, axis=1) + jnp.sum(own[None, :] * direction * direction, axis=1)

time: 300 us -> 235 us (0.78)
  Pallas kernels: 251 us -> 206 us
  local copies, waits for them, and re-layouts: 15.2 us -> 5.74 us
  other arithmetic: 31 us -> 23.3 us
    pallas_call x3, Pallas kernels: 99.1 us -> 72.2 us  [scatter(): pl.pallas_call(functools.partial(scatter_kernel, rows, cols), out_shape=(...]
    pallas_call x3, Pallas kernels: 118 us -> 99.1 us  [gather(): pl.pallas_call(functools.partial(gather_kernel, rows, cols), out_shape=(j...]
    slice x5 -> x0, local copies, waits for them, and re-layouts: 4.86 us -> none  [the longest x1 2.4 us: shards(): column_image[:, :rhs + 8]]
    reduce_sum x2 -> x0, other arithmetic: 4.18 us -> none  [the longest x1 2.97 us: shards(): jnp.sum(right * right, axis=1)[:, None, :]]
where the time goes in v2:
time: 235 us; the launch traced here: 236 us
  Pallas kernels  206 us (88%)
  other arithmetic  23.3 us (10%)
  local copies, waits for them, and re-layouts  5.74 us (2%)
    pallas_call x3, Pallas kernels, gather(): pl.pallas_call(functools.partial(gather_kernel, rows, cols), out_shape=(j...  99.1 us
    pallas_call x3, Pallas kernels, scatter(): pl.pallas_call(functools.partial(scatter_kernel, rows, cols), out_shape=(...  72.2 us
    pallas_call x3, Pallas kernels, sweep(): pl.pallas_call(functools.partial(sweep_kernel, rhs, start), grid=(count,)...  25.6 us
    pallas_call x1, Pallas kernels, build(): pl.pallas_call(functools.partial(build_kernel, depth), grid=(count,), out...  8.79 us

profile of v2, /device:TPU:0, one launch (start us, length us, event | category | flops | bytes accessed | tf_op | source)
XLA Modules:
  0.0 235.6 jit_solution(1734451777357094011)
XLA Ops:
  0.6 1.3 copy.12
  2.0 0.7 convert_element_type.12
  2.7 1.7 fusion.x
  4.4 1.0 fusion.8
  5.4 0.6 pad.24.s
  6.0 47.6 %shard_map.77 = (f32[4,136,512]{2,1,0:T(8,128)}, f32[8,136,512]{2,1,0:T(8,128)}, f32[8,128]{1,0:T(8,128)}) custom-call(f32[136,512]{1,0:T(8,128)} %fusion.x, f32[8,128]{1,0:T(8,128)} %pad.24.s), custom_call_target="tpu_custom_call" | custom-call | tf_op jit(solution)/shard_map/pallas_call | solution.py:192
  53.6 8.8 %shard_map.78 = (bf16[8,512,512]{2,1,0:T(8,128)(2,1)}, bf16[8,512,512]{2,1,0:T(8,128)(2,1)}) custom-call(s32[8,3]{1,0:T(8,128)} %bitcast.22, f32[4,136,512]{2,1,0:T(8,128)} %get-tuple-element.29.by_col.row_values, f32[8,136,512]{2,1,0:T(8,128)} %get-tuple-element.30.by_row.column_values, f32[2,2]{1,0:T(2,128)} %coupling.1), custom_call_target="tpu_custom_call" | custom-call | tf_op jit(solution)/shard_map/pallas_call | solution.py:253
  62.4 9.0 %shard_map.79 = (f32[4,72,512]{2,1,0:T(8,128)}, f32[8,72,512]{2,1,0:T(8,128)}, f32[64,128]{1,0:T(8,128)}) custom-call(s32[8,3]{1,0:T(8,128)} %bitcast.23, f32[4,136,512]{2,1,0:T(8,128)} %get-tuple-element.29.by_col.row_values, f32[8,136,512]{2,1,0:T(8,128)} %get-tuple-element.30.by_row.column_values, bf16[8,512,512]{2,1,0:T(8,128)(2,1)} %get-tuple-element.31.high, ...), custom_call_target="tpu_custom_call" | custom-call | tf_op jit(solution)/shard_map/pallas_call | solution.py:321
  71.4 0.9 reduce_sum.82
  72.3 0.6 pad.25.s
  72.9 28.3 %shard_map.80 = (f32[72,512]{1,0:T(8,128)}, f32[8,128]{1,0:T(8,128)}) custom-call(f32[4,72,512]{2,1,0:T(8,128)} %get-tuple-element.33.by_col, f32[8,72,512]{2,1,0:T(8,128)} %get-tuple-element.34.by_row, f32[8,128]{1,0:T(8,128)} %pad.25.s), custom_call_target="tpu_custom_call" | custom-call | tf_op jit(solution)/shard_map/pallas_call | solution.py:211
  101.2 0.7 slice.32
  101.9 0.0 copy-done.7
  101.9 0.7 fusion.9
  102.7 0.0 copy-done.2
  102.7 1.7 multiply_reduce_fusion.1
  104.4 0.6 pad.26.s
  105.0 26.5 %shard_map.81 = (f32[4,64,512]{2,1,0:T(8,128)}, f32[8,64,512]{2,1,0:T(8,128)}, f32[8,128]{1,0:T(8,128)}) custom-call(f32[64,512]{1,0:T(8,128)} %get-tuple-element.61.x, f32[8,128]{1,0:T(8,128)} %pad.26.s), custom_call_target="tpu_custom_call" | custom-call | tf_op jit(solution)/shard_map/pallas_call | solution.py:192
  131.5 0.0 copy-start.5
  131.6 0.8 divide_bitcast_fusion.1
  132.3 2.1 multiply_add_fusion.3.row_values
  134.5 0.0 copy-done.5
  134.5 2.5 %multiply_add_fusion.1.column_values = f32[8,64,512]{2,1,0:T(8,128)} fusion(f32[8,64,512]{2,1,0:T(8,128)S(1)} %copy-done.5, f32[8,136,512]{2,1,0:T(8,128)} %get-tuple-element.30.by_row.column_values, f32[64]{0:T(128)S(1)} %divide_bitcast_fusion.1), kind=kLoop, calls=%fused_computation.1 | loop fusion | flops 524288 | bytes 3145984 | tf_op jit(solution)/shard_map/add | solution.py:380
  136.9 8.3 %shard_map.82 = (f32[4,64,512]{2,1,0:T(8,128)}, f32[8,64,512]{2,1,0:T(8,128)}, f32[64,128]{1,0:T(8,128)}) custom-call(s32[8,3]{1,0:T(8,128)} %bitcast.24, f32[4,64,512]{2,1,0:T(8,128)} %multiply_add_fusion.3.row_values, f32[8,64,512]{2,1,0:T(8,128)} %multiply_add_fusion.1.column_values, bf16[8,512,512]{2,1,0:T(8,128)(2,1)} %get-tuple-element.31.high, ...), custom_call_target="tpu_custom_call" | custom-call | tf_op jit(solution)/shard_map/pallas_call | solution.py:321
  145.3 0.0 copy-start
  145.3 1.0 reduce_sum.85
  146.3 0.0 copy-done.3
  146.3 0.2 fusion.2
  146.5 0.6 pad.27.s
  147.1 22.9 %shard_map.83 = (f32[64,512]{1,0:T(8,128)}, f32[8,128]{1,0:T(8,128)}) custom-call(f32[4,64,512]{2,1,0:T(8,128)} %get-tuple-element.41.by_col, f32[8,64,512]{2,1,0:T(8,128)} %get-tuple-element.42.by_row, f32[8,128]{1,0:T(8,128)} %pad.27.s), custom_call_target="tpu_custom_call" | custom-call | tf_op jit(solution)/shard_map/pallas_call | solution.py:211
  170.0 0.7 fusion.10
  170.6 1.7 multiply_reduce_fusion
  172.4 0.6 pad.28.s
  173.0 25.0 %shard_map.84 = (f32[4,64,512]{2,1,0:T(8,128)}, f32[8,64,512]{2,1,0:T(8,128)}, f32[8,128]{1,0:T(8,128)}) custom-call(f32[64,512]{1,0:T(8,128)} %get-tuple-element.57.x, f32[8,128]{1,0:T(8,128)} %pad.28.s), custom_call_target="tpu_custom_call" | custom-call | tf_op jit(solution)/shard_map/pallas_call | solution.py:192
  198.0 0.0 copy-start.6
  198.0 0.8 divide_bitcast_fusion
  198.8 0.0 copy-done.1
  198.8 2.0 multiply_add_fusion.2.row_values
  200.8 0.0 copy-done
  200.8 1.3 multiply_add_fusion.column_values
  202.1 8.3 %shard_map.85 = (f32[4,64,512]{2,1,0:T(8,128)}, f32[8,64,512]{2,1,0:T(8,128)}, f32[64,128]{1,0:T(8,128)}) custom-call(s32[8,3]{1,0:T(8,128)} %bitcast.25, f32[4,64,512]{2,1,0:T(8,128)} %multiply_add_fusion.2.row_values, f32[8,64,512]{2,1,0:T(8,128)} %multiply_add_fusion.column_values, bf16[8,512,512]{2,1,0:T(8,128)(2,1)} %get-tuple-element.31.high, ...), custom_call_target="tpu_custom_call" | custom-call | tf_op jit(solution)/shard_map/pallas_call | solution.py:321
  210.4 0.9 reduce_sum.88
  211.3 0.0 copy-done.4
  211.3 0.2 fusion.5
  211.5 0.6 pad.29.s
  212.1 21.1 %shard_map.86 = (f32[64,512]{1,0:T(8,128)}, f32[8,128]{1,0:T(8,128)}) custom-call(f32[4,64,512]{2,1,0:T(8,128)} %get-tuple-element.49.by_col, f32[8,64,512]{2,1,0:T(8,128)} %get-tuple-element.50.by_row, f32[8,128]{1,0:T(8,128)} %pad.29.s), custom_call_target="tpu_custom_call" | custom-call | tf_op jit(solution)/shard_map/pallas_call | solution.py:211
  233.1 0.7 fusion.11
  233.8 1.7 fusion.7
  (10 shorter events, 0.0 us)
Async XLA Ops:
  62.3 39.6 %copy-start.7 = (f32[512]{0:T(512)S(1)}, f32[512]{0:T(512)}, u32[]{:S(2)}) copy-start(f32[512]{0:T(512)} %param.9) | copy-start | bytes 6148
  62.4 40.3 %copy-start.2 = (f32[64,512]{1,0:T(8,128)S(1)}, f32[64,512]{1,0:T(8,128)}, u32[]{:S(2)}) copy-start(f32[64,512]{1,0:T(8,128)} %param.6) | copy-start | bytes 393220
  131.5 2.9 %copy-start.5 = (f32[8,64,512]{2,1,0:T(8,128)S(1)}, f32[8,64,512]{2,1,0:T(8,128)}, u32[]{:S(2)}) copy-start(f32[8,64,512]{2,1,0:T(8,128)} %get-tuple-element.40) | copy-start | bytes 3145732
  136.9 9.3 %copy-start.3 = (f32[64,512]{1,0:T(8,128)S(1)}, f32[64,512]{1,0:T(8,128)}, u32[]{:S(2)}) copy-start(f32[64,512]{1,0:T(8,128)} %get-tuple-element.61.x) | copy-start | bytes 393220
  145.3 53.5 %copy-start.1 = (f32[4,64,512]{2,1,0:T(8,128)S(1)}, f32[4,64,512]{2,1,0:T(8,128)}, u32[]{:S(2)}) copy-start(f32[4,64,512]{2,1,0:T(8,128)} %multiply_add_fusion.3.row_values) | copy-start | bytes 1572868
  145.3 55.5 %copy-start = (f32[8,64,512]{2,1,0:T(8,128)S(1)}, f32[8,64,512]{2,1,0:T(8,128)}, u32[]{:S(2)}) copy-start(f32[8,64,512]{2,1,0:T(8,128)} %multiply_add_fusion.1.column_values) | copy-start | bytes 3145732
  198.0 2.8 %copy-start.6 = (f32[8,64,512]{2,1,0:T(8,128)S(1)}, f32[8,64,512]{2,1,0:T(8,128)}, u32[]{:S(2)}) copy-start(f32[8,64,512]{2,1,0:T(8,128)} %get-tuple-element.48) | copy-start | bytes 3145732
  202.1 9.1 %copy-start.4 = (f32[64,512]{1,0:T(8,128)S(1)}, f32[64,512]{1,0:T(8,128)}, u32[]{:S(2)}) copy-start(f32[64,512]{1,0:T(8,128)} %get-tuple-element.57.x) | copy-start | bytes 393220

commit v3 on v2

--- a/solution.py
+++ b/solution.py
@@ -311,6 +311,35 @@
         dots[...] += amount
 
 
+def turn_kernel(rhs, slots, beta, row_fresh, column_fresh, row_old, column_old, high, low,
+                row_image, column_image, dots, row_values, column_values):
+    @pl.when(pl.program_id(0) == 0)
+    def _():
+        factor = beta[:, :1]
+        start = row_old.shape[1] - rhs
+        for a in range(row_old.shape[0]):
+            row_values[a] = row_fresh[a] + factor * row_old[a, start:]
+        for b in range(column_old.shape[0]):
+            column_values[b] = column_fresh[b] + factor * column_old[b, start:]
+
+    sweep_kernel(rhs, 0, slots, row_values, column_values, high, low,
+                 row_image, column_image, dots)
+
+
+def turn(rhs, slots, beta, row_fresh, column_fresh, row_old, column_old, high, low):
+    count, tile = high.shape[0], high.shape[1]
+    whole = lambda shape: pl.BlockSpec(shape, lambda i: (0,) * len(shape))
+    tiles = pl.BlockSpec((1, tile, tile), lambda i: (i, 0, 0))
+    shapes = (row_fresh.shape, column_fresh.shape, (rhs, 128), row_fresh.shape, column_fresh.shape)
+    return pl.pallas_call(
+        functools.partial(turn_kernel, rhs),
+        grid=(count,),
+        out_shape=tuple(jax.ShapeDtypeStruct(shape, jnp.float32) for shape in shapes),
+        in_specs=[SMEM] + [VMEM] * 5 + [tiles, tiles],
+        out_specs=tuple(whole(shape) for shape in shapes),
+    )(slots, beta, row_fresh, column_fresh, row_old, column_old, high, low)
+
+
 def sweep(rhs, start, kept, slots, row_values, column_values, high, low):
     count, tile = high.shape[0], high.shape[1]
     whole = lambda shape: pl.BlockSpec(shape, lambda i: (0,) * len(shape))
@@ -343,8 +372,7 @@
     norm_now = total[0, :rhs]
 
     high, low = build(depth, slots, by_col, by_row, coupling)
-    row_values = by_col[:, depth + 8:]
-    column_values = by_row[:, depth + 8:]
+    row_values, column_values = by_col, by_row
 
     increment = jnp.zeros_like(innovations)
     residual = innovations
@@ -357,8 +385,9 @@
             )
             own = obs_error
         else:
-            row_image, column_image, dots = sweep(
-                rhs, 0, rhs, slots, row_values, column_values, high, low
+            row_image, column_image, dots, row_values, column_values = turn(
+                rhs, slots, jnp.broadcast_to(beta, (rhs, 128)), by_col, by_row,
+                row_values, column_values, high, low,
             )
             own = diagonal
         part = jnp.sum(dots, axis=1) + jnp.sum(own[None, :] * direction * direction, axis=1)
@@ -376,8 +405,6 @@
             norm_next = total[0, :rhs]
             beta = (norm_next / norm_now)[:, None]
             direction = residual + beta * direction
-            row_values = by_col + beta * row_values
-            column_values = by_row + beta * column_values
             norm_now = norm_next
     return (increment, residual)
 

time: 235 us -> 234 us (level); the launches traced: 236 us -> 230 us
  other arithmetic: 23.3 us -> 16 us
    pallas_call x0 -> x2, Pallas kernels: none -> 21.2 us  [turn(): pl.pallas_call(functools.partial(turn_kernel, rhs), grid=(count,), out_sh...]
    pallas_call x3 -> x1, Pallas kernels: 25.6 us -> 9.57 us  [sweep(): pl.pallas_call(functools.partial(sweep_kernel, rhs, start), grid=(count,)...]
    add x4 -> x0, other arithmetic: 7.94 us -> none  [the longest x2 4.14 us: shards(): row_values = by_col + beta * row_values]
    pallas_call x3, Pallas kernels: 72.2 us -> 66 us  [scatter(): pl.pallas_call(functools.partial(scatter_kernel, rows, cols), out_shape=(...]
where the time goes in v3:
time: 234 us; the launch traced here: 230 us
  Pallas kernels  206 us (88%)
  other arithmetic  16 us (7%)
  local copies, waits for them, and re-layouts  7.11 us (3%)
    pallas_call x3, Pallas kernels, gather(): pl.pallas_call(functools.partial(gather_kernel, rows, cols), out_shape=(j...  98.9 us
    pallas_call x3, Pallas kernels, scatter(): pl.pallas_call(functools.partial(scatter_kernel, rows, cols), out_shape=(...  66 us
    pallas_call x2, Pallas kernels, turn(): pl.pallas_call(functools.partial(turn_kernel, rhs), grid=(count,), out_sh...  21.2 us
    pallas_call x1, Pallas kernels, build(): pl.pallas_call(functools.partial(build_kernel, depth), grid=(count,), out...  10.6 us
    pallas_call x1, Pallas kernels, sweep(): pl.pallas_call(functools.partial(sweep_kernel, rhs, start), grid=(count,)...  9.57 us

profile of v3, /device:TPU:0, one launch (start us, length us, event | category | flops | bytes accessed | tf_op | source)
XLA Modules:
  0.0 230.1 jit_solution(9362498718393622775)
XLA Ops:
  0.6 1.0 fusion.8
  1.7 0.7 convert_element_type.12
  2.4 0.6 pad.24.s
  3.0 1.3 copy.12
  4.3 1.7 fusion.x
  6.0 47.5 %shard_map.77 = (f32[4,136,512]{2,1,0:T(8,128)}, f32[8,136,512]{2,1,0:T(8,128)}, f32[8,128]{1,0:T(8,128)}) custom-call(f32[136,512]{1,0:T(8,128)} %fusion.x, f32[8,128]{1,0:T(8,128)} %pad.24.s), custom_call_target="tpu_custom_call" | custom-call | tf_op jit(solution)/shard_map/pallas_call | solution.py:192
  53.5 10.6 %shard_map.78 = (bf16[8,512,512]{2,1,0:T(8,128)(2,1)}, bf16[8,512,512]{2,1,0:T(8,128)(2,1)}) custom-call(s32[8,3]{1,0:T(8,128)} %bitcast.22, f32[4,136,512]{2,1,0:T(8,128)} %get-tuple-element.31.by_col.row_values.row_old, f32[8,136,512]{2,1,0:T(8,128)} %get-tuple-element.32.by_row.column_values.column_old, f32[2,2]{1,0:T(2,128)} %coupling.1), custom_call_target="tpu_custom_call" | custom-call | tf_op jit(solution)/shard_map/pallas_call | solution.py:253
  64.2 0.0 copy-start.3
  64.2 0.0 copy-start
  64.2 9.6 %shard_map.79 = (f32[4,72,512]{2,1,0:T(8,128)}, f32[8,72,512]{2,1,0:T(8,128)}, f32[64,128]{1,0:T(8,128)}) custom-call(s32[8,3]{1,0:T(8,128)} %bitcast.23, f32[4,136,512]{2,1,0:T(8,128)} %get-tuple-element.31.by_col.row_values.row_old, f32[8,136,512]{2,1,0:T(8,128)} %get-tuple-element.32.by_row.column_values.column_old, ...), custom_call_target="tpu_custom_call" | custom-call | tf_op jit(solution)/shard_map/pallas_call | solution.py:350
  73.7 0.9 reduce_sum.82
  74.6 0.6 pad.25.s
  75.2 23.4 %shard_map.80 = (f32[72,512]{1,0:T(8,128)}, f32[8,128]{1,0:T(8,128)}) custom-call(f32[4,72,512]{2,1,0:T(8,128)} %get-tuple-element.35.by_col, f32[8,72,512]{2,1,0:T(8,128)} %get-tuple-element.36.by_row, f32[8,128]{1,0:T(8,128)} %pad.25.s), custom_call_target="tpu_custom_call" | custom-call | tf_op jit(solution)/shard_map/pallas_call | solution.py:211
  98.6 0.7 fusion.9
  99.3 0.7 slice.26
  100.0 0.0 copy-done.3
  100.0 0.0 copy-done
  100.0 1.7 multiply_reduce_fusion.1
  101.8 0.6 pad.26.s
  102.4 25.9 %shard_map.81 = (f32[4,64,512]{2,1,0:T(8,128)}, f32[8,64,512]{2,1,0:T(8,128)}, f32[8,128]{1,0:T(8,128)}) custom-call(f32[64,512]{1,0:T(8,128)} %get-tuple-element.65.x, f32[8,128]{1,0:T(8,128)} %pad.26.s), custom_call_target="tpu_custom_call" | custom-call | tf_op jit(solution)/shard_map/pallas_call | solution.py:192
  128.3 0.7 divide_bitcast_fusion.1
  129.0 0.7 broadcast_in_dim.15.beta
  129.7 0.0 copy-start.1
  129.7 10.9 %shard_map.82 = (f32[4,64,512]{2,1,0:T(8,128)}, f32[8,64,512]{2,1,0:T(8,128)}, f32[64,128]{1,0:T(8,128)}, f32[4,64,512]{2,1,0:T(8,128)}, f32[8,64,512]{2,1,0:T(8,128)}) custom-call(s32[8,3]{1,0:T(8,128)} %bitcast.24, f32[64,128]{1,0:T(8,128)} %broadcast_in_dim.15.beta, f32[4,64,512]{2,1,0:T(8,128)} %get-tuple-element.41.row_fresh, ...), custom_call_target="tpu_custom_call" | custom-call | tf_op jit(solution)/shard_map/pallas_call | solution.py:334
  140.6 0.9 reduce_sum.85
  141.5 0.0 copy-done.1
  141.5 0.2 fusion.2
  141.7 0.6 pad.27.s
  142.3 20.2 %shard_map.83 = (f32[64,512]{1,0:T(8,128)}, f32[8,128]{1,0:T(8,128)}) custom-call(f32[4,64,512]{2,1,0:T(8,128)} %get-tuple-element.43.by_col, f32[8,64,512]{2,1,0:T(8,128)} %get-tuple-element.44.by_row, f32[8,128]{1,0:T(8,128)} %pad.27.s), custom_call_target="tpu_custom_call" | custom-call | tf_op jit(solution)/shard_map/pallas_call | solution.py:211
  162.5 0.7 fusion.10
  163.2 1.7 multiply_reduce_fusion
  164.9 0.6 pad.28.s
  165.5 25.5 %shard_map.84 = (f32[4,64,512]{2,1,0:T(8,128)}, f32[8,64,512]{2,1,0:T(8,128)}, f32[8,128]{1,0:T(8,128)}) custom-call(f32[64,512]{1,0:T(8,128)} %get-tuple-element.61.x, f32[8,128]{1,0:T(8,128)} %pad.28.s), custom_call_target="tpu_custom_call" | custom-call | tf_op jit(solution)/shard_map/pallas_call | solution.py:192
  191.0 0.7 divide_bitcast_fusion
  191.7 1.1 fusion.5
  192.8 0.7 broadcast_in_dim.17.beta
  193.5 0.0 copy-start.2
  193.5 10.2 %shard_map.85 = (f32[4,64,512]{2,1,0:T(8,128)}, f32[8,64,512]{2,1,0:T(8,128)}, f32[64,128]{1,0:T(8,128)}, f32[4,64,512]{2,1,0:T(8,128)}, f32[8,64,512]{2,1,0:T(8,128)}) custom-call(s32[8,3]{1,0:T(8,128)} %bitcast.25, f32[64,128]{1,0:T(8,128)} %broadcast_in_dim.17.beta, f32[4,64,512]{2,1,0:T(8,128)} %get-tuple-element.49.row_fresh, ...), custom_call_target="tpu_custom_call" | custom-call | tf_op jit(solution)/shard_map/pallas_call | solution.py:334
  203.7 0.9 reduce_sum.88
  204.6 0.6 pad.29.s
  205.2 22.4 %shard_map.86 = (f32[64,512]{1,0:T(8,128)}, f32[8,128]{1,0:T(8,128)}) custom-call(f32[4,64,512]{2,1,0:T(8,128)} %get-tuple-element.53.by_col, f32[8,64,512]{2,1,0:T(8,128)} %get-tuple-element.54.by_row, f32[8,128]{1,0:T(8,128)} %pad.29.s), custom_call_target="tpu_custom_call" | custom-call | tf_op jit(solution)/shard_map/pallas_call | solution.py:211
  227.7 0.7 fusion.11
  228.4 0.0 copy-done.2
  228.4 1.7 fusion.7
  (4 shorter events, 0.0 us)
Async XLA Ops:
  64.2 35.8 %copy-start.3 = (f32[512]{0:T(512)S(1)}, f32[512]{0:T(512)}, u32[]{:S(2)}) copy-start(f32[512]{0:T(512)} %param.9) | copy-start | bytes 6148
  64.2 35.9 %copy-start = (f32[64,512]{1,0:T(8,128)S(1)}, f32[64,512]{1,0:T(8,128)}, u32[]{:S(2)}) copy-start(f32[64,512]{1,0:T(8,128)} %param.6) | copy-start | bytes 393220
  129.7 11.8 %copy-start.1 = (f32[64,512]{1,0:T(8,128)S(1)}, f32[64,512]{1,0:T(8,128)}, u32[]{:S(2)}) copy-start(f32[64,512]{1,0:T(8,128)} %get-tuple-element.65.x) | copy-start | bytes 393220
  193.5 34.9 %copy-start.2 = (f32[64,512]{1,0:T(8,128)S(1)}, f32[64,512]{1,0:T(8,128)}, u32[]{:S(2)}) copy-start(f32[64,512]{1,0:T(8,128)} %get-tuple-element.61.x) | copy-start | bytes 393220
